TPU v7x, 256 devices: a whole 4x4x8 slice. The times are simulated.
256 devices in a mesh: vol: 64 (over z, y, core), dsg: 4 (over x).
Axes of the slice: x: 4, y: 4, z: 8, core: 2. Of those that a mesh axis runs over, the one named last changes fastest.
Arguments:
- fields: float32 [262144, 128], P('vol'), may hold values from -6 to 6
- far_geom: float32 [8, 131072], P(None, ('vol', 'dsg')), may hold values from -6 to 6, as said below
- far_block: int32 [131072, 1], P(('vol', 'dsg')), may hold values from 0 to 63; in each aligned block of 512 rows (0 to 511, 512 to 1023, ...) at most 20 rows name the same one
- far_cell: int32 [131072], P(('vol', 'dsg')), may hold values from 0 to 4095
- far_patch: int32 [131072], P(('vol', 'dsg')), may hold values from 0 to 95, as said below
- near_geom: float32 [8, 524288], P(None, ('vol', 'dsg')), may hold values from -6 to 6, as said below
- near_cell: int32 [524288], P(('vol', 'dsg')), may hold values from 0 to 4095
- near_patch: int32 [524288], P(('vol', 'dsg')), may hold values from 0 to 95, as said below
- adjacency: int32 [96, 4], replicated, may hold values from -1 to 95, as said below
Outputs:
- far_density: float32 [131072], P(('vol', 'dsg'))
- design_grad: float32 [96, 64, 64], P('dsg')
Inputs may be any that keep to these rules, and one draw needn't show every extreme that they name: `far_geom`: rows 0-2 and 6-7 lie in [0, 1). `near_geom`: rows 0-2 and 6-7 lie in [0, 1). `far_block`: the 512 far points of one device name each block at most 20 times. `far_patch`: the far and near points of one device lie on at most 4 design patches, the same set for both. `near_patch`: the far and near points of one device lie on at most 4 design patches, the same set for both. -1 marks a free side; where adjacency[k, s] = m >= 0, adjacency[m, s xor 1] = k.
All inputs are finite; a program needn't handle non-finite values.
Results may differ from a plain program's by a relative error of at most 0.0003.
Values sent between devices are 32-bit elements; how exact they have to be, the bound alone decides.
A program may use at most 128 MiB of HBM per device.

v0:
```python
import jax
import jax.numpy as jnp
import numpy as np
from jax import lax
from jax.sharding import PartitionSpec as P

CTRL = 64
PATCH_GRP = 4
SMOOTH_ITERS = 3
PENALTY = 4.0
SMOOTHING = 16.0
FLIPPED = np.array([1, 0, 3, 2], dtype=np.int32)


def bernstein(position):
    complement = 1.0 - position
    values = jnp.stack(
        [
            complement * complement * complement,
            3.0 * position * complement * complement,
            3.0 * position * position * complement,
            position * position * position,
        ]
    )
    slopes = jnp.stack(
        [
            -3.0 * complement * complement,
            3.0 * complement * complement - 6.0 * position * complement,
            6.0 * position * complement - 3.0 * position * position,
            3.0 * position * position,
        ]
    )
    return (values, slopes)


def tensor_basis(factor_x, factor_y, factor_z):
    product = factor_x[:, None, None, :] * factor_y[None, :, None, :] * factor_z[None, None, :, :]
    return product.reshape(-1, factor_x.shape[-1])


def evaluate(columns, coords):
    value_x, slope_x = bernstein(coords[0])
    value_y, slope_y = bernstein(coords[1])
    value_z, slope_z = bernstein(coords[2])
    basis_set = [
        tensor_basis(value_x, value_y, value_z),
        tensor_basis(slope_x, value_y, value_z),
        tensor_basis(value_x, slope_y, value_z),
        tensor_basis(value_x, value_y, slope_z),
    ]
    half_width = columns.shape[0] // 2
    state_part = columns[:half_width]
    adjoint_part = columns[half_width:]
    results = [jnp.sum(state_part * basis_kind, 0) for basis_kind in basis_set]
    results = results + [jnp.sum(adjoint_part * basis_kind, 0) for basis_kind in basis_set]
    return jnp.stack(results)


def density(values, normals):
    grad_state = values[1:4]
    grad_adjoint = values[5:8]
    normal_sq = jnp.sum(normals * normals, 0)
    inner_sum = jnp.sum(grad_state * grad_adjoint, 0)
    along_state = jnp.sum(grad_state * normals, 0)
    along_adjoint = jnp.sum(grad_adjoint * normals, 0)
    return (
        normal_sq * inner_sum
        - 2.0 * along_state * along_adjoint
        + PENALTY * normal_sq * values[0] * values[4]
    )


def spline_weights(param, span_count):
    scaled = param * span_count
    first_span = jnp.clip(jnp.floor(scaled), 0, span_count - 1)
    offset_in = scaled - first_span
    complement = 1.0 - offset_in
    cubed = offset_in * offset_in * offset_in
    squared = offset_in * offset_in
    weights = jnp.stack(
        [
            complement * complement * complement / 6.0,
            (3.0 * cubed - 6.0 * squared + 4.0) / 6.0,
            (-3.0 * cubed + 3.0 * squared + 3.0 * offset_in + 1.0) / 6.0,
            cubed / 6.0,
        ]
    )
    return (first_span.astype(jnp.int32), weights)


def spline_matrix(param, control):
    start, weights = spline_weights(param, control - 3)
    columns = jnp.arange(control, dtype=jnp.int32)
    matrix = jnp.zeros((param.shape[0], control), jnp.float32)
    for offset in range(4):
        matrix = matrix + jnp.where(
            (start + offset)[:, None] == columns[None, :], weights[offset][:, None], 0.0
        )
    return matrix


def local_grid(strength, spline_params, patch_ids, slot_ids, slot_live, control):
    weights_s = spline_matrix(spline_params[0], control)
    weights_t = spline_matrix(spline_params[1], control)
    selector = ((patch_ids[:, None] == slot_ids[None, :]) & slot_live[None, :]).astype(jnp.float32)
    left = ((selector * strength[:, None])[:, :, None] * weights_s[:, None, :]).reshape(
        strength.shape[0], -1
    )
    result = jnp.einsum(
        "na,nb->ab",
        left,
        weights_t,
        precision=lax.Precision.HIGHEST,
        preferred_element_type=jnp.float32,
    )
    return result.reshape(slot_ids.shape[0], control, control)


def edge_table(iterate):
    return jnp.stack([iterate[:, 0, :], iterate[:, -1, :], iterate[:, :, 0], iterate[:, :, -1]], 1)


def lookup(edge_rows, neighbours):
    total_rows = edge_rows.shape[0] * 4
    wanted = (neighbours * 4 + FLIPPED[None, :]).reshape(-1)
    present = (neighbours >= 0).reshape(-1)
    selector = (
        (wanted[:, None] == jnp.arange(total_rows, dtype=jnp.int32)[None, :]) & present[:, None]
    ).astype(jnp.float32)
    picked = jnp.dot(
        selector,
        edge_rows.reshape(total_rows, -1),
        precision=lax.Precision.HIGHEST,
        preferred_element_type=jnp.float32,
    )
    return picked.reshape(neighbours.shape[0], 4, -1)


def apply_operator(iterate, halo_rows):
    patch_count, edge_size = (iterate.shape[0], iterate.shape[1])
    padded = jnp.zeros((patch_count, edge_size + 2, edge_size + 2), iterate.dtype)
    padded = padded.at[:, 1:-1, 1:-1].set(iterate)
    padded = padded.at[:, 0, 1:-1].set(halo_rows[:, 0])
    padded = padded.at[:, -1, 1:-1].set(halo_rows[:, 1])
    padded = padded.at[:, 1:-1, 0].set(halo_rows[:, 2])
    padded = padded.at[:, 1:-1, -1].set(halo_rows[:, 3])
    beside = padded[:, :-2, 1:-1] + padded[:, 2:, 1:-1] + padded[:, 1:-1, :-2] + padded[:, 1:-1, 2:]
    return iterate + SMOOTHING * (4.0 * iterate - beside)


def precondition(residual):
    patch_count, edge_size = (residual.shape[0], residual.shape[1])
    below_diag = jnp.full((patch_count, edge_size), -SMOOTHING, residual.dtype).at[:, 0].set(0.0)
    main_diag = jnp.full((patch_count, edge_size), 1.0 + 2.0 * SMOOTHING, residual.dtype)
    above_diag = jnp.full((patch_count, edge_size), -SMOOTHING, residual.dtype).at[:, -1].set(0.0)
    along_rows = lax.linalg.tridiagonal_solve(below_diag, main_diag, above_diag, residual)
    along_cols = lax.linalg.tridiagonal_solve(
        below_diag, main_diag, above_diag, jnp.swapaxes(along_rows, 1, 2)
    )
    return jnp.swapaxes(along_cols, 1, 2)


def keep_table(edge_rows):
    return edge_rows


def smooth(summed, neighbours, edges_of):
    iterate = precondition(summed)
    for sweep_index in range(SMOOTH_ITERS):
        halo_rows = lookup(edges_of(edge_table(iterate)), neighbours)
        iterate = iterate + precondition(summed - apply_operator(iterate, halo_rows))
    return iterate


def per_device(
    fields, far_geom, far_block, far_cell, far_patch, near_geom, near_cell, near_patch, adjacency
):
    vol_count = lax.axis_size("vol")
    far_count = far_cell.shape[0]
    capacity = 5 * far_count // (2 * vol_count)
    patches = adjacency.shape[0]
    control = CTRL
    group = PATCH_GRP
    patch_range = jnp.arange(patches, dtype=jnp.int32)
    present = jnp.any(near_patch[:, None] == patch_range[None, :], 0)
    present = present | jnp.any(far_patch[:, None] == patch_range[None, :], 0)
    rank = jnp.cumsum(present.astype(jnp.int32)) - 1
    matches = present[None, :] & (rank[None, :] == jnp.arange(group, dtype=jnp.int32)[:, None])
    slot_ids = jnp.sum(matches.astype(jnp.int32) * patch_range[None, :], 1)
    slot_live = jnp.any(matches, 1)
    near_count = near_cell.shape[0]
    block_len = min(4096, near_count)
    blocks = near_count // block_len

    def near_block(carried, inputs):
        geom_part, cells_part, patch_part = inputs
        rows = jnp.take(fields, cells_part, axis=0).T
        strength = density(evaluate(rows, geom_part[0:3]), geom_part[3:6])
        return (
            carried
            + local_grid(strength, geom_part[6:8], patch_part, slot_ids, slot_live, control),
            None,
        )

    start_grid = jnp.zeros((group, control, control), jnp.float32)
    grid_local, unused = lax.scan(
        near_block,
        start_grid,
        (
            near_geom.reshape(8, blocks, block_len).transpose(1, 0, 2),
            near_cell.reshape(blocks, block_len),
            near_patch.reshape(blocks, block_len),
        ),
    )
    target = far_block[:, 0]
    onehot_dest = (target[:, None] == jnp.arange(vol_count, dtype=jnp.int32)[None, :]).astype(
        jnp.int32
    )
    before = jnp.cumsum(onehot_dest, 0) - onehot_dest
    slot_rank = jnp.sum(before * onehot_dest, 1)
    slot_of = target * capacity + slot_rank
    request = jnp.zeros((1, vol_count * capacity), jnp.int32).at[0, slot_of].set(far_cell)
    request = request.reshape(1, vol_count, capacity)
    incoming = lax.all_to_all(request, "vol", split_axis=1, concat_axis=1, tiled=True)
    picked = jnp.take(fields, incoming.reshape(-1), axis=0).T
    picked = picked.reshape(fields.shape[1], incoming.shape[1], incoming.shape[2])
    replies = lax.all_to_all(picked, "vol", split_axis=1, concat_axis=1, tiled=True)
    placed = jnp.zeros((3, vol_count * capacity), jnp.float32).at[:, slot_of].set(far_geom[0:3])
    slot_values = evaluate(replies.reshape(replies.shape[0], -1), placed)
    far_values = jnp.take(slot_values, slot_of, axis=1)
    far_strength = density(far_values, far_geom[3:6])
    grid_local = grid_local + local_grid(
        far_strength, far_geom[6:8], far_patch, slot_ids, slot_live, control
    )
    placing = ((patch_range[:, None] == slot_ids[None, :]) & slot_live[None, :]).astype(jnp.float32)
    owner_count = lax.axis_size("dsg")
    per_owner = patches // owner_count
    owner_index = lax.axis_index("dsg")
    grid_whole = jnp.dot(
        placing,
        grid_local.reshape(group, -1),
        precision=lax.Precision.HIGHEST,
        preferred_element_type=jnp.float32,
    )
    summed = lax.psum(grid_whole, ("vol", "dsg")).reshape(patches, control, control)
    design = smooth(summed, adjacency, keep_table)
    design = lax.dynamic_slice_in_dim(design, owner_index * per_owner, per_owner, 0)
    return (far_strength, design)


def solution(mesh):
    return jax.shard_map(
        per_device,
        mesh=mesh,
        in_specs=(
            P("vol", None),
            P(None, ("vol", "dsg")),
            P(("vol", "dsg"), None),
            P(("vol", "dsg")),
            P(("vol", "dsg")),
            P(None, ("vol", "dsg")),
            P(("vol", "dsg")),
            P(("vol", "dsg")),
            P(),
        ),
        out_specs=(P(("vol", "dsg")), P("dsg", None, None)),
        check_vma=False,
    )
```

profile of v0, /device:TPU:2, one launch (start us, length us, event | category | flops | bytes accessed | tf_op | source)
XLA Modules:
  0.0 598.5 jit_solution(6945396377052510805)
XLA Ops:
  11.5 2.6 scatter_custom_fusion
  14.9 12.1 %all-to-all-start = ((s32[1,64,20]{2,0,1:T(1,128)}), s32[1,64,20]{2,0,1:T(1,128)S(1)}, u32[]{:S(2)}, u32[]{:S(2)}) async-start(s32[1,64,20]{2,0,1:T(1,128)} %bitcast.5), calls=%async_computation | async-start | bytes 65536 | tf_op jit(solution)/shard_map/all_to_all | solution.py:224
  27.0 1.7 slice_multiply_fusion.4
  41.7 1.9 scatter_custom_fusion.1
  55.8 2.0 mul.70953
  57.8 2.4 copy.7291
  60.2 2.0 mul.70965
  62.2 2.4 copy.7292
  64.6 2.0 mul.70978
  66.6 2.4 copy.7296
  68.9 4.6 mul.70848
  73.6 3.5 copy.7280
  77.1 4.4 mul.70860
  81.5 3.6 copy.7281
  85.1 4.4 mul.70872
  89.6 3.6 copy.7282
  93.1 3.8 mul.70882
  96.9 3.5 copy.7283
  100.7 7.6 %gather_fusion.2 = f32[2048,128]{1,0:T(8,128)} fusion(f32[4096,128]{1,0:T(8,128)S(1)} %copy-done, s32[2048]{0:T(1024)S(1)} %get-tuple-element.1882), kind=kCustom, calls=%fused_computation.2 | custom fusion | bytes 2105344 | tf_op jit(solution)/shard_map/while/body/eval_jaxpr/jit(_take)/gather | solution.py:197
  108.4 3.1 gather_fusion
  115.1 10.4 %all-to-all-start.1 = ((f32[128,64,20]{0,2,1:T(8,128)}), f32[128,64,20]{0,2,1:T(8,128)S(1)}, u32[]{:S(2)}, u32[]{:S(2)}) async-start(f32[128,64,20]{0,2,1:T(8,128)} %reshape.315135), calls=%async_computation.1 | async-start | bytes 1572864 | tf_op jit(solution)/shard_map/all_to_all | solution.py:227
  127.9 2.6 multiply_reduce_fusion.7
  130.8 18.1 %all-to-all-done.1 = f32[128,64,20]{0,2,1:T(8,128)S(1)} async-done(((f32[128,64,20]{0,2,1:T(8,128)}), f32[128,64,20]{0,2,1:T(8,128)S(1)}, u32[]{:S(2)}, u32[]{:S(2)}) %all-to-all-start.1) | async-done | bytes 655392 | tf_op jit(solution)/shard_map/all_to_all | solution.py:227
  148.8 3.8 multiply_reduce_fusion.8
  156.9 2.0 fusion.16
  159.1 3.1 fusion.83
  163.0 257.5 %all-reduce.6.cloned.1.call-done = f32[96,64,64]{0,2,1:T(8,128)} async-done(((f32[96,64,64]{0,2,1:T(8,128)}), f32[96,64,64]{0,2,1:T(8,128)}) %all-reduce.6.cloned.1.call-update) | async-done | bytes 1572880 | tf_op jit(solution)/shard_map/psum | solution.py:245
  420.5 1.7 slice_bitcast_fusion.7
  437.5 4.8 multiply_subtract_fusion.370
  442.4 9.9 %concatenate.199 = f32[63,96,64]{1,0,2:T(8,128)S(1)} concatenate(f32[1,96,64]{1,0,2:T(1,128)} %get-tuple-element.1225, f32[1,96,64]{1,0,2:T(1,128)} %get-tuple-element.1226, f32[1,96,64]{1,0,2:T(1,128)} %get-tuple-element.1227, f32[1,96,64]{1,0,2:T(1,128)} %get-tuple-element.1228, f32[1,96,64]{1,0,2:T(1,128)} %get-tuple-element.1229, f32[1,96,64]{1,0,2:T(1,128)} %get-tuple-element.1230, ...), dimensions={0} | concatenate | bytes 3096576 | tf_op jit(solution)/shard_map/vmap()/concatenate | solution.py:156
  458.6 2.2 scatter.69
  463.7 3.3 fusion.11
  469.4 2.7 multiply_subtract_fusion.308
  476.5 2.7 broadcast_multiply_fusion.14
  490.0 2.2 scatter.76
  494.9 3.0 fusion.7
  506.5 1.7 subtract_multiply_fusion.142
  515.1 4.7 multiply_subtract_fusion.124
  519.8 15.6 %concatenate.207 = f32[63,96,64]{1,0,2:T(8,128)} concatenate(f32[1,96,64]{1,0,2:T(1,128)S(1)} %get-tuple-element.820, f32[1,96,64]{1,0,2:T(1,128)S(1)} %get-tuple-element.821, f32[1,96,64]{1,0,2:T(1,128)S(1)} %get-tuple-element.822, f32[1,96,64]{1,0,2:T(1,128)} %get-tuple-element.823, f32[1,96,64]{1,0,2:T(1,128)} %get-tuple-element.824, f32[1,96,64]{1,0,2:T(1,128)} %get-tuple-element.825, ...), dimensions={0} | concatenate | bytes 3096576 | tf_op jit(solution)/shard_map/vmap()/concatenate | solution.py:156
  535.4 2.0 fusion.12
  543.6 2.2 scatter.85
  546.4 3.0 fusion.3
  550.7 1.8 subtract_multiply_fusion.100
  552.6 4.3 multiply_subtract_fusion.62
  569.4 4.9 multiply_subtract_fusion
  574.4 9.8 %concatenate.211 = f32[63,96,64]{1,0,2:T(8,128)S(1)} concatenate(f32[1,96,64]{1,0,2:T(1,128)S(1)} %get-tuple-element.656, f32[1,96,64]{1,0,2:T(1,128)S(1)} %get-tuple-element.657, f32[1,96,64]{1,0,2:T(1,128)S(1)} %get-tuple-element.658, f32[1,96,64]{1,0,2:T(1,128)} %get-tuple-element.659, f32[1,96,64]{1,0,2:T(1,128)} %get-tuple-element.660, f32[1,96,64]{1,0,2:T(1,128)} %get-tuple-element.661, ...), dimensions={0} | concatenate | bytes 3096576 | tf_op jit(solution)/shard_map/vmap()/concatenate | solution.py:156
  585.8 2.5 dynamic-slice_add_fusion
  588.2 3.2 copy.8826
  (878 shorter events, 118.6 us)
Async XLA Ops:
  7.2 93.6 %copy-start = (f32[4096,128]{1,0:T(8,128)S(1)}, f32[4096,128]{1,0:T(8,128)}, u32[]{:S(2)}) copy-start(f32[4096,128]{1,0:T(8,128)} %param.58) | copy-start | bytes 6291460
  11.5 30.1 %copy-start.118 = (s32[512,1]{0,1:T(1,128)}, s32[512,1]{0,1:T(1,128)S(1)}, u32[]{:S(2)}) copy-start(s32[512,1]{0,1:T(1,128)S(1)} %get-tuple-element.1367) | copy-start | bytes 6148
  14.9 85.7 %all-to-all-start = ((s32[1,64,20]{2,0,1:T(1,128)}), s32[1,64,20]{2,0,1:T(1,128)S(1)}, u32[]{:S(2)}, u32[]{:S(2)}) async-start(s32[1,64,20]{2,0,1:T(1,128)} %bitcast.5), calls=%async_computation | async-start | bytes 65536 | tf_op jit(solution)/shard_map/all_to_all | solution.py:224
  48.9 3.5 copy-start.88
  48.9 3.5 copy-start.89
  48.9 4.5 copy-start.119
  93.1 7.3 %copy-start.102 = (f32[3,512]{1,0:T(4,128)S(1)}, f32[3,512]{1,0:T(4,128)}, u32[]{:S(2)}) copy-start(f32[3,512]{1,0:T(4,128)} %get-tuple-element.1815) | copy-start | bytes 18436
  96.9 3.8 copy-start.101
  112.9 13.2 %copy-start.109 = (pred[2048]{0:T(1024)(128)(4,1)S(1)}, pred[2048]{0:T(1024)(128)(4,1)}, u32[]{:S(2)}) copy-start(pred[2048]{0:T(1024)(128)(4,1)} %compare_and_fusion) | copy-start | bytes 6148
  115.1 12.6 %copy-start.8 = (f32[64,2048]{0,1:T(8,128)S(1)}, f32[64,2048]{0,1:T(8,128)}, u32[]{:S(2)}) copy-start(f32[64,2048]{0,1:T(8,128)} %copy.7291) | copy-start | bytes 1572868
  115.1 33.7 %all-to-all-start.1 = ((f32[128,64,20]{0,2,1:T(8,128)}), f32[128,64,20]{0,2,1:T(8,128)S(1)}, u32[]{:S(2)}, u32[]{:S(2)}) async-start(f32[128,64,20]{0,2,1:T(8,128)} %reshape.315135), calls=%async_computation.1 | async-start | bytes 1572864 | tf_op jit(solution)/shard_map/all_to_all | solution.py:227
  125.6 294.9 %all-reduce.6.cloned.1.call-start = ((), (), s32[]{:S(2)}) async-start(), calls=%async_computation.2 | async-start | bytes 4194304 | tf_op jit(solution)/shard_map/psum | solution.py:245
  130.8 24.3 %copy-start.133 = (pred[512]{0:T(512)(128)(4,1)S(1)}, pred[512]{0:T(512)(128)(4,1)}, u32[]{:S(2)}) copy-start(pred[512]{0:T(512)(128)(4,1)} %get-tuple-element.1366) | copy-start | bytes 1540
  152.6 3.4 copy-start.121
  152.6 3.5 copy-start.87
  152.6 3.5 copy-start.134
  152.7 3.5 copy-start.135
  152.7 3.5 copy-start.136
  152.7 3.5 copy-start.137
  152.7 3.5 copy-start.138
  152.7 3.5 copy-start.139
  152.7 3.5 copy-start.140
  152.7 3.5 copy-start.141
  152.7 4.1 copy-start.79
  152.7 4.1 copy-start.123
  152.7 4.1 copy-start.124
  152.8 4.1 copy-start.125
  152.8 4.1 copy-start.126
  152.8 4.1 copy-start.127
  152.8 4.1 copy-start.128
  152.8 4.1 copy-start.129
  152.8 4.1 copy-start.130
  156.1 6.2 %copy-start.122 = (f32[512]{0:T(512)}, f32[512]{0:T(512)S(1)}, u32[]{:S(2)}) copy-start(f32[512]{0:T(512)S(1)} %multiply_add_fusion.2) | copy-start | bytes 6148
  159.1 3.8 copy-start.120
  159.1 3.8 copy-start.142
  431.2 11.1 %copy-start.80 = (f32[96,64]{0,1:T(8,128)}, f32[96,64]{0,1:T(8,128)S(1)}, u32[]{:S(2)}) copy-start(f32[96,64]{0,1:T(8,128)S(1)} %get-tuple-element.1210) | copy-start | bytes 73732
  431.2 11.1 %copy-start.83 = (f32[96,64]{0,1:T(8,128)}, f32[96,64]{0,1:T(8,128)S(1)}, u32[]{:S(2)}) copy-start(f32[96,64]{0,1:T(8,128)S(1)} %get-tuple-element.1211) | copy-start | bytes 73732
  431.2 21.0 %copy-start.75 = (f32[96,64]{0,1:T(8,128)}, f32[96,64]{0,1:T(8,128)S(1)}, u32[]{:S(2)}) copy-start(f32[96,64]{0,1:T(8,128)S(1)} %get-tuple-element.1202) | copy-start | bytes 73732
  437.3 5.0 copy-start.11
  437.4 4.9 copy-start.15
  437.4 4.9 copy-start.19
  437.4 4.9 copy-start.23
  437.4 4.9 copy-start.27
  437.5 4.9 copy-start.31
  519.8 15.6 %copy-start.5 = (f32[96,64,64]{0,2,1:T(8,128)S(1)}, f32[96,64,64]{0,2,1:T(8,128)}, u32[]{:S(2)}) copy-start(f32[96,64,64]{0,2,1:T(8,128)} %copy-done.4) | copy-start | bytes 4718596
  519.8 15.6 %copy-start.86 = (f32[96,64]{0,1:T(8,128)S(1)}, f32[96,64]{0,1:T(8,128)}, u32[]{:S(2)}) copy-start(f32[96,64]{0,1:T(8,128)} %get-tuple-element.800) | copy-start | bytes 73732
  574.4 9.8 %copy-start.85 = (f32[96,64]{0,1:T(8,128)S(1)}, f32[96,64]{0,1:T(8,128)}, u32[]{:S(2)}) copy-start(f32[96,64]{0,1:T(8,128)} %get-tuple-element.636) | copy-start | bytes 73732
  585.8 5.6 copy-start.1
  (98 other events, 177.4 us)
Sparse Core Ops, SparseCore 0:
  162.4 258.0 all-reduce.5
where the time goes:
time: 609 us; the launch traced here: 599 us
  waiting for transfers between devices  276 us (45%)
  local copies, waits for them, and re-layouts  155 us (25%)
  other arithmetic  114 us (19%)
  starting transfers between devices  23 us (4%)
  between operations  20.4 us (3%)
  matrix products  10.6 us (2%)
    psum x1, waiting for transfers between devices, per_device(): lax.psum(grid_whole, ('vol', 'dsg')).reshape(patches, control, control)  258 us
    mul x16, local copies, waits for them, and re-layouts, tensor_basis(): factor_x[:, None, None, :] * factor_y[None, :, None, :]  47 us
    sub x37, other arithmetic, precondition(): lax.linalg.tridiagonal_solve(below_diag, main_diag, above_diag, residual)  42 us
    concatenate x3, local copies, waits for them, and re-layouts, precondition(): lax.linalg.tridiagonal_solve(below_diag, main_diag, above_diag, residual)  35.3 us
    all_to_all x1, waiting for transfers between devices, per_device(): lax.all_to_all(picked, 'vol', split_axis=1, concat_axis=1, tiled=True)  18.1 us
    unnamed x515, local copies, waits for them, and re-layouts  16 us
  transfers between devices with their start and end apart: 3, of which 2 were waited for; matrix products, arithmetic and copies ran while one was open for 13% of the time, Pallas kernels for 0%

commit v1 on v0

--- a/solution.py
+++ b/solution.py
@@ -242,7 +242,7 @@
         precision=lax.Precision.HIGHEST,
         preferred_element_type=jnp.float32,
     )
-    summed = lax.psum(grid_whole, ("vol", "dsg")).reshape(patches, control, control)
+    summed = lax.psum(lax.psum(grid_whole, "vol"), "dsg").reshape(patches, control, control)
     design = smooth(summed, adjacency, keep_table)
     design = lax.dynamic_slice_in_dim(design, owner_index * per_owner, per_owner, 0)
     return (far_strength, design)

time: 609 us -> 601 us (0.987)
  the two profiles are of different devices: /device:TPU:2 before, /device:TPU:1 now
where the time goes in v1:
time: 601 us; the launch traced here: 590 us
  waiting for transfers between devices  264 us (44%)
  local copies, waits for them, and re-layouts  158 us (26%)
  other arithmetic  114 us (19%)
  starting transfers between devices  24.2 us (4%)
  between operations  20.3 us (3%)
  matrix products  9.41 us (2%)
    psum x1, waiting for transfers between devices, per_device(): lax.psum(grid_whole, 'vol')  183 us
    psum x1, waiting for transfers between devices, per_device(): lax.psum(lax.psum(grid_whole, 'vol'), 'dsg')  63.5 us
    mul x16, local copies, waits for them, and re-layouts, tensor_basis(): factor_x[:, None, None, :] * factor_y[None, :, None, :]  47.3 us
    sub x37, other arithmetic, precondition(): lax.linalg.tridiagonal_solve(below_diag, main_diag, above_diag, residual)  41.8 us
    concatenate x3, local copies, waits for them, and re-layouts, precondition(): lax.linalg.tridiagonal_solve(below_diag, main_diag, above_diag, residual)  35.3 us
    all_to_all x1, waiting for transfers between devices, per_device(): lax.all_to_all(picked, 'vol', split_axis=1, concat_axis=1, tiled=True)  17.8 us
    unnamed x515, local copies, waits for them, and re-layouts  16 us
    all_to_all x1, starting transfers between devices, per_device(): lax.all_to_all(request, 'vol', split_axis=1, concat_axis=1, tiled=True)  13.2 us
  transfers between devices with their start and end apart: 4, of which 3 were waited for; matrix products, arithmetic and copies ran while one was open for 13% of the time, Pallas kernels for 0%

profile of v1, /device:TPU:1, one launch (start us, length us, event | category | flops | bytes accessed | tf_op | source)
XLA Modules:
  0.0 590.0 jit_solution(3506495703910926080)
XLA Ops:
  11.5 2.6 scatter_custom_fusion
  14.9 13.2 %all-to-all-start = ((s32[1,64,20]{2,0,1:T(1,128)}), s32[1,64,20]{2,0,1:T(1,128)S(1)}, u32[]{:S(2)}, u32[]{:S(2)}) async-start(s32[1,64,20]{2,0,1:T(1,128)} %bitcast.5), calls=%async_computation | async-start | bytes 65536 | tf_op jit(solution)/shard_map/all_to_all | solution.py:224
  42.7 1.9 scatter_custom_fusion.1
  56.8 2.0 mul.70953
  58.8 2.4 copy.7291
  61.2 2.0 mul.70965
  63.2 2.4 copy.7292
  65.6 2.0 mul.70978
  67.6 2.4 copy.7296
  70.0 4.9 mul.70848
  74.9 3.5 copy.7280
  78.4 4.4 mul.70860
  82.9 3.6 copy.7281
  86.4 4.4 mul.70872
  90.9 3.6 copy.7282
  94.5 3.8 mul.70882
  98.2 3.5 copy.7283
  102.1 7.6 %gather_fusion.2 = f32[2048,128]{1,0:T(8,128)} fusion(f32[4096,128]{1,0:T(8,128)S(1)} %copy-done, s32[2048]{0:T(1024)S(1)} %get-tuple-element.1882), kind=kCustom, calls=%fused_computation.2 | custom fusion | bytes 2105344 | tf_op jit(solution)/shard_map/while/body/eval_jaxpr/jit(_take)/gather | solution.py:197
  109.7 3.1 gather_fusion
  116.5 10.4 %all-to-all-start.1 = ((f32[128,64,20]{0,2,1:T(8,128)}), f32[128,64,20]{0,2,1:T(8,128)S(1)}, u32[]{:S(2)}, u32[]{:S(2)}) async-start(f32[128,64,20]{0,2,1:T(8,128)} %reshape.315135), calls=%async_computation.1 | async-start | bytes 1572864 | tf_op jit(solution)/shard_map/all_to_all | solution.py:227
  129.0 2.6 multiply_reduce_fusion.7
  131.9 17.8 %all-to-all-done.1 = f32[128,64,20]{0,2,1:T(8,128)S(1)} async-done(((f32[128,64,20]{0,2,1:T(8,128)}), f32[128,64,20]{0,2,1:T(8,128)S(1)}, u32[]{:S(2)}, u32[]{:S(2)}) %all-to-all-start.1) | async-done | bytes 655392 | tf_op jit(solution)/shard_map/all_to_all | solution.py:227
  149.7 3.8 multiply_reduce_fusion.8
  157.8 2.0 fusion.16
  159.9 1.9 fusion.83
  162.3 182.8 %all-reduce.7.cloned.1.call-done = f32[96,4096]{1,0:T(8,128)} async-done(((f32[96,4096]{1,0:T(8,128)}), f32[96,4096]{1,0:T(8,128)}) %all-reduce.7.cloned.1.call-update) | async-done | bytes 1572880 | tf_op jit(solution)/shard_map/psum | solution.py:245
  345.1 2.8 copy.7298
  348.7 63.5 %all-reduce.9.cloned.1.call-done = f32[96,64,64]{0,2,1:T(8,128)} async-done(((f32[96,64,64]{0,2,1:T(8,128)}), f32[96,64,64]{0,2,1:T(8,128)}) %all-reduce.9.cloned.1.call-update) | async-done | bytes 1572880 | tf_op jit(solution)/shard_map/psum | solution.py:245
  429.0 4.8 multiply_subtract_fusion.370
  433.9 9.9 %concatenate.199 = f32[63,96,64]{1,0,2:T(8,128)S(1)} concatenate(f32[1,96,64]{1,0,2:T(1,128)} %get-tuple-element.1225, f32[1,96,64]{1,0,2:T(1,128)} %get-tuple-element.1226, f32[1,96,64]{1,0,2:T(1,128)} %get-tuple-element.1227, f32[1,96,64]{1,0,2:T(1,128)} %get-tuple-element.1228, f32[1,96,64]{1,0,2:T(1,128)} %get-tuple-element.1229, f32[1,96,64]{1,0,2:T(1,128)} %get-tuple-element.1230, ...), dimensions={0} | concatenate | bytes 3096576 | tf_op jit(solution)/shard_map/vmap()/concatenate | solution.py:156
  450.1 2.2 scatter.69
  455.2 3.3 fusion.11
  460.9 2.7 multiply_subtract_fusion.308
  468.0 2.7 broadcast_multiply_fusion.14
  481.4 2.2 scatter.76
  486.4 3.0 fusion.7
  497.9 1.7 subtract_multiply_fusion.142
  506.5 4.7 multiply_subtract_fusion.124
  511.2 15.6 %concatenate.207 = f32[63,96,64]{1,0,2:T(8,128)} concatenate(f32[1,96,64]{1,0,2:T(1,128)S(1)} %get-tuple-element.820, f32[1,96,64]{1,0,2:T(1,128)S(1)} %get-tuple-element.821, f32[1,96,64]{1,0,2:T(1,128)S(1)} %get-tuple-element.822, f32[1,96,64]{1,0,2:T(1,128)} %get-tuple-element.823, f32[1,96,64]{1,0,2:T(1,128)} %get-tuple-element.824, f32[1,96,64]{1,0,2:T(1,128)} %get-tuple-element.825, ...), dimensions={0} | concatenate | bytes 3096576 | tf_op jit(solution)/shard_map/vmap()/concatenate | solution.py:156
  526.8 2.0 fusion.12
  535.0 2.2 scatter.85
  537.8 3.0 fusion.3
  542.1 1.8 subtract_multiply_fusion.100
  544.0 4.3 multiply_subtract_fusion.62
  560.9 4.9 multiply_subtract_fusion
  565.8 9.8 %concatenate.211 = f32[63,96,64]{1,0,2:T(8,128)S(1)} concatenate(f32[1,96,64]{1,0,2:T(1,128)S(1)} %get-tuple-element.656, f32[1,96,64]{1,0,2:T(1,128)S(1)} %get-tuple-element.657, f32[1,96,64]{1,0,2:T(1,128)S(1)} %get-tuple-element.658, f32[1,96,64]{1,0,2:T(1,128)} %get-tuple-element.659, f32[1,96,64]{1,0,2:T(1,128)} %get-tuple-element.660, f32[1,96,64]{1,0,2:T(1,128)} %get-tuple-element.661, ...), dimensions={0} | concatenate | bytes 3096576 | tf_op jit(solution)/shard_map/vmap()/concatenate | solution.py:156
  577.2 2.5 dynamic-slice_add_fusion
  579.7 3.2 copy.8826
  (882 shorter events, 122.1 us)
Async XLA Ops:
  7.2 94.9 %copy-start = (f32[4096,128]{1,0:T(8,128)S(1)}, f32[4096,128]{1,0:T(8,128)}, u32[]{:S(2)}) copy-start(f32[4096,128]{1,0:T(8,128)} %param.58) | copy-start | bytes 6291460
  11.5 31.2 %copy-start.118 = (s32[512,1]{0,1:T(1,128)}, s32[512,1]{0,1:T(1,128)S(1)}, u32[]{:S(2)}) copy-start(s32[512,1]{0,1:T(1,128)S(1)} %get-tuple-element.1367) | copy-start | bytes 6148
  14.9 87.0 %all-to-all-start = ((s32[1,64,20]{2,0,1:T(1,128)}), s32[1,64,20]{2,0,1:T(1,128)S(1)}, u32[]{:S(2)}, u32[]{:S(2)}) async-start(s32[1,64,20]{2,0,1:T(1,128)} %bitcast.5), calls=%async_computation | async-start | bytes 65536 | tf_op jit(solution)/shard_map/all_to_all | solution.py:224
  49.9 3.5 copy-start.88
  49.9 3.5 copy-start.89
  50.0 4.5 copy-start.119
  94.4 7.3 %copy-start.102 = (f32[3,512]{1,0:T(4,128)S(1)}, f32[3,512]{1,0:T(4,128)}, u32[]{:S(2)}) copy-start(f32[3,512]{1,0:T(4,128)} %get-tuple-element.1815) | copy-start | bytes 18436
  98.2 3.8 copy-start.101
  114.2 12.9 %copy-start.109 = (pred[2048]{0:T(1024)(128)(4,1)S(1)}, pred[2048]{0:T(1024)(128)(4,1)}, u32[]{:S(2)}) copy-start(pred[2048]{0:T(1024)(128)(4,1)} %compare_and_fusion) | copy-start | bytes 6148
  116.5 12.4 %copy-start.8 = (f32[64,2048]{0,1:T(8,128)S(1)}, f32[64,2048]{0,1:T(8,128)}, u32[]{:S(2)}) copy-start(f32[64,2048]{0,1:T(8,128)} %copy.7291) | copy-start | bytes 1572868
  116.5 33.2 %all-to-all-start.1 = ((f32[128,64,20]{0,2,1:T(8,128)}), f32[128,64,20]{0,2,1:T(8,128)S(1)}, u32[]{:S(2)}, u32[]{:S(2)}) async-start(f32[128,64,20]{0,2,1:T(8,128)} %reshape.315135), calls=%async_computation.1 | async-start | bytes 1572864 | tf_op jit(solution)/shard_map/all_to_all | solution.py:227
  126.9 218.2 %all-reduce.7.cloned.1.call-start = ((), (), s32[]{:S(2)}) async-start(), calls=%async_computation.2 | async-start | bytes 3145728 | tf_op jit(solution)/shard_map/psum | solution.py:245
  131.9 24.0 %copy-start.133 = (pred[512]{0:T(512)(128)(4,1)S(1)}, pred[512]{0:T(512)(128)(4,1)}, u32[]{:S(2)}) copy-start(pred[512]{0:T(512)(128)(4,1)} %get-tuple-element.1366) | copy-start | bytes 1540
  153.5 3.5 copy-start.87
  153.5 3.5 copy-start.134
  153.5 3.5 copy-start.135
  153.5 3.5 copy-start.136
  153.5 3.5 copy-start.137
  153.5 3.5 copy-start.138
  153.5 3.5 copy-start.139
  153.5 3.5 copy-start.140
  153.5 3.5 copy-start.141
  153.5 4.1 copy-start.79
  153.6 4.1 copy-start.123
  153.6 4.1 copy-start.124
  153.6 4.1 copy-start.125
  153.6 4.1 copy-start.126
  153.6 4.1 copy-start.127
  153.6 4.1 copy-start.128
  153.6 4.1 copy-start.129
  153.6 4.1 copy-start.130
  156.9 5.0 copy-start.122
  161.9 186.7 %copy-start.120 = (s32[96,4]{0,1:T(4,128)S(1)}, s32[96,4]{0,1:T(4,128)}, u32[]{:S(2)}) copy-start(s32[96,4]{0,1:T(4,128)} %param.66) | copy-start | bytes 4612
  161.9 186.7 %copy-start.142 = (s32[4]{0:T(128)S(1)}, s32[4]{0:T(128)}, u32[]{:S(2)}) copy-start(s32[4]{0:T(128)} %constant.5725) | copy-start | bytes 52
  161.9 250.3 %all-reduce.9.cloned.1.call-start = ((), (), s32[]{:S(2)}) async-start(), calls=%async_computation.3 | async-start | bytes 4194304 | tf_op jit(solution)/shard_map/psum | solution.py:245
  422.9 10.9 %copy-start.80 = (f32[96,64]{0,1:T(8,128)}, f32[96,64]{0,1:T(8,128)S(1)}, u32[]{:S(2)}) copy-start(f32[96,64]{0,1:T(8,128)S(1)} %get-tuple-element.1210) | copy-start | bytes 73732
  422.9 10.9 %copy-start.83 = (f32[96,64]{0,1:T(8,128)}, f32[96,64]{0,1:T(8,128)S(1)}, u32[]{:S(2)}) copy-start(f32[96,64]{0,1:T(8,128)S(1)} %get-tuple-element.1211) | copy-start | bytes 73732
  422.9 20.9 %copy-start.75 = (f32[96,64]{0,1:T(8,128)}, f32[96,64]{0,1:T(8,128)S(1)}, u32[]{:S(2)}) copy-start(f32[96,64]{0,1:T(8,128)S(1)} %get-tuple-element.1202) | copy-start | bytes 73732
  428.9 5.0 copy-start.11
  428.9 4.9 copy-start.15
  428.9 4.9 copy-start.19
  428.9 4.9 copy-start.23
  429.0 4.9 copy-start.27
  429.0 4.9 copy-start.31
  511.2 15.6 %copy-start.5 = (f32[96,64,64]{0,2,1:T(8,128)S(1)}, f32[96,64,64]{0,2,1:T(8,128)}, u32[]{:S(2)}) copy-start(f32[96,64,64]{0,2,1:T(8,128)} %copy-done.4) | copy-start | bytes 4718596
  511.2 15.6 %copy-start.86 = (f32[96,64]{0,1:T(8,128)S(1)}, f32[96,64]{0,1:T(8,128)}, u32[]{:S(2)}) copy-start(f32[96,64]{0,1:T(8,128)} %get-tuple-element.800) | copy-start | bytes 73732
  565.8 9.8 %copy-start.85 = (f32[96,64]{0,1:T(8,128)S(1)}, f32[96,64]{0,1:T(8,128)}, u32[]{:S(2)}) copy-start(f32[96,64]{0,1:T(8,128)} %get-tuple-element.636) | copy-start | bytes 73732
  577.2 5.6 copy-start.1
  (99 other events, 180.8 us)
Sparse Core Ops, SparseCore 0:
  162.0 183.1 all-reduce.6
  348.1 64.0 all-reduce.8
